TPU v7x, 128 devices: a whole 4x4x4 slice. The times are simulated.
128 devices in a mesh: tok: 16 (over z, y), mdl: 8 (over x, core).
Axes of the slice: x: 4, y: 4, z: 4, core: 2. Of those that a mesh axis runs over, the one named last changes fastest.
Arguments:
- tokens: bfloat16 [4096, 5120], P('tok'), may hold values from -32 to 32
- norm_gain: bfloat16 [5120], replicated, may hold values from 0.099609375 to 1.8984375
- w_query: bfloat16 [5120, 4096], P(None, 'mdl'), may hold values from -0.078125 to 0.078125
- w_key: bfloat16 [5120, 1024], P(None, 'mdl'), may hold values from -0.3125 to 0.3125
- w_value: bfloat16 [5120, 1024], P(None, 'mdl'), may hold values from -0.078125 to 0.078125
- w_out: bfloat16 [4096, 5120], P('mdl'), may hold values from -0.09375 to 0.09375
- prompt_keys: bfloat16 [6, 4096, 8, 128], P(None, 'tok', 'mdl'), may hold values from -6 to 6
- prompt_values: bfloat16 [6, 4096, 8, 128], P(None, 'tok', 'mdl'), may hold values from -24 to 24
- cache_keys: bfloat16 [128, 2048, 8, 128], P('tok', None, 'mdl'), may hold values from -6 to 6
- cache_values: bfloat16 [128, 2048, 8, 128], P('tok', None, 'mdl'), may hold values from -24 to 24
- cache_length: int32 [128], P('tok'), may hold values from 1 to 2048, as said below
- request_group: int32 [128], replicated, may hold values from 0 to 5
- ancestors: int32 [128, 32, 32], P('tok'), may hold values from 0 to 1, as said below
- accepted: int32 [128, 8], P('tok'), may hold values from -1 to 31, as said below
Outputs:
- attention_out: bfloat16 [4096, 5120], P('tok', 'mdl')
- compact_rows: bfloat16 [128, 8, 5120], P('tok', None, 'mdl')
Inputs may be any that keep to these rules, and one draw needn't show every extreme that they name: `cache_length`: some request has exactly 2048 live slots. ancestors[r, a, b] is 1 where tree slot b is slot a itself or an ancestor of it in request r's draft tree, else 0; each tree has one root, and slots are in no particular order. Entry k of request r is the tree slot of the accepted path's node at depth k, from the root on, for k below the path's length, and -1 after it; a path holds 1 to 8 nodes, and some request's path holds 8.
All inputs are finite; a program needn't handle non-finite values.
Results may differ from a plain program's by a relative error of at most 0.017.
Values may be sent and summed in bfloat16 or wider, within the bound.
No kernel may reach another device: no remote copies, remote signals or barrier semaphores. Data moves between devices by JAX's collectives and lax.ppermute only.
A program may use at most 128 MiB of HBM per device.

v0:
```python
import jax
import jax.numpy as jnp
from jax import lax
from jax.sharding import PartitionSpec as P

PROMPT = 4096
THETA = 100000000.0
EPS = 1e-05


def rotate_pairs(vectors, positions):
    middle = vectors.shape[-1] // 2
    exponent = jnp.arange(middle, dtype=jnp.float32) * (2.0 / vectors.shape[-1])
    inverse = jnp.power(jnp.float32(THETA), -exponent)
    angles = positions.astype(jnp.float32)[:, None] * inverse[None, :]
    cosine = jnp.cos(angles)[:, None, :]
    sine_part = jnp.sin(angles)[:, None, :]
    leading = vectors[..., :middle]
    trailing = vectors[..., middle:]
    return jnp.concatenate(
        [leading * cosine - trailing * sine_part, trailing * cosine + leading * sine_part], axis=-1
    )


def slice_attention(grouped, chosen_keys, chosen_values, slice_rows, factor):
    pieces = chosen_keys.shape[1] // slice_rows
    layout = (chosen_keys.shape[0], pieces, slice_rows, chosen_keys.shape[2], chosen_keys.shape[3])
    keys_split = chosen_keys.reshape(layout)
    values_split = chosen_values.reshape(layout)
    scores = (
        jnp.einsum("ntkgd,nsckd->ntkgsc", grouped, keys_split, preferred_element_type=jnp.float32)
        * factor
    )
    weights = jnp.exp(scores)
    totals = jnp.sum(weights, axis=5)
    numerator = jnp.einsum(
        "ntkgsc,nsckd->ntkgsd",
        weights.astype(jnp.bfloat16),
        values_split,
        preferred_element_type=jnp.float32,
    )
    outputs = (numerator / totals[..., None]).astype(jnp.bfloat16)
    return (outputs, totals)


def cache_block(grouped, key_block, value_block, lengths, factor):
    scores = (
        jnp.einsum("ntkgd,nckd->ntkgc", grouped, key_block, preferred_element_type=jnp.float32)
        * factor
    )
    places = jnp.arange(key_block.shape[1], dtype=jnp.int32)
    live = places[None, :] < lengths[:, None]
    weights = jnp.where(live[:, None, None, None, :], jnp.exp(scores), 0.0)
    numerator = jnp.einsum(
        "ntkgc,nckd->ntkgd",
        weights.astype(jnp.bfloat16),
        value_block,
        preferred_element_type=jnp.float32,
    )
    return (numerator, jnp.sum(weights, axis=4))


def shards(
    tokens,
    norm_gain,
    w_query,
    w_key,
    w_value,
    w_out,
    prompt_keys,
    prompt_values,
    cache_keys,
    cache_values,
    cache_length,
    request_group,
    ancestors,
    accepted,
):
    requests = cache_length.shape[0]
    tree_size = ancestors.shape[1]
    head_dim = prompt_keys.shape[3]
    key_heads = prompt_keys.shape[2]
    query_heads = w_query.shape[1] // head_dim
    group_size = query_heads // key_heads
    slice_rows = prompt_keys.shape[1]
    factor = head_dim ** (-0.5)
    rows_local = tokens.shape[0]
    wide = tokens.astype(jnp.float32)
    normed = (
        wide
        * lax.rsqrt(jnp.mean(wide * wide, axis=1, keepdims=True) + EPS)
        * norm_gain.astype(jnp.float32)
    ).astype(jnp.bfloat16)
    queries = jnp.dot(normed, w_query, preferred_element_type=jnp.float32).reshape(
        rows_local, query_heads, head_dim
    )
    new_keys = jnp.dot(normed, w_key, preferred_element_type=jnp.float32).reshape(
        rows_local, key_heads, head_dim
    )
    new_values = (
        jnp.dot(normed, w_value, preferred_element_type=jnp.float32)
        .astype(jnp.bfloat16)
        .reshape(requests, tree_size, key_heads, head_dim)
    )
    depth = jnp.sum(ancestors, axis=2) - 1
    positions = (PROMPT + cache_length[:, None] + depth).reshape(rows_local)
    queries = rotate_pairs(queries, positions).astype(jnp.bfloat16)
    new_keys = (
        rotate_pairs(new_keys, positions)
        .astype(jnp.bfloat16)
        .reshape(requests, tree_size, key_heads, head_dim)
    )
    grouped = queries.reshape(requests, tree_size, key_heads, group_size, head_dim)
    first_request = lax.axis_index("tok") * requests
    own_groups = lax.dynamic_slice_in_dim(request_group, first_request, requests)
    chosen_keys = jnp.take(
        lax.all_gather(prompt_keys, "tok", axis=1, tiled=True), own_groups, axis=0
    )
    chosen_values = jnp.take(
        lax.all_gather(prompt_values, "tok", axis=1, tiled=True), own_groups, axis=0
    )
    outputs, totals = slice_attention(grouped, chosen_keys, chosen_values, slice_rows, factor)
    weighted = jnp.sum(totals[..., None] * outputs.astype(jnp.float32), axis=4)
    prompt_total = jnp.sum(totals, axis=4)
    cache_part, cache_total = cache_block(grouped, cache_keys, cache_values, cache_length, factor)
    tree_scores = (
        jnp.einsum("ntkgd,nmkd->ntkgm", grouped, new_keys, preferred_element_type=jnp.float32)
        * factor
    )
    tree_weights = jnp.where(ancestors[:, :, None, None, :] > 0, jnp.exp(tree_scores), 0.0)
    tree_part = jnp.einsum(
        "ntkgm,nmkd->ntkgd",
        tree_weights.astype(jnp.bfloat16),
        new_values,
        preferred_element_type=jnp.float32,
    )
    denominator = prompt_total + cache_total + jnp.sum(tree_weights, axis=4)
    merged = (weighted + cache_part + tree_part) / denominator[..., None]
    attended = merged.astype(jnp.bfloat16).reshape(rows_local, query_heads * head_dim)
    projected = jnp.dot(attended, w_out, preferred_element_type=jnp.float32)
    attention_out = lax.psum_scatter(
        projected.astype(jnp.bfloat16), "mdl", scatter_dimension=1, tiled=True
    )
    columns = attention_out.shape[1]
    column_start = lax.axis_index("mdl") * columns
    residual = lax.dynamic_slice_in_dim(tokens, column_start, columns, 1).astype(
        jnp.float32
    ) + attention_out.astype(jnp.float32)
    rows_index = (
        jnp.arange(requests, dtype=jnp.int32)[:, None] * tree_size + jnp.maximum(accepted, 0)
    ).reshape(requests * accepted.shape[1])
    picked = jnp.take(residual, rows_index, axis=0).reshape(requests, accepted.shape[1], columns)
    compact_rows = jnp.where(accepted[:, :, None] >= 0, picked, 0.0).astype(jnp.bfloat16)
    return (attention_out, compact_rows)


def solution(mesh):
    placed = (
        P("tok", None),
        P(),
        P(None, "mdl"),
        P(None, "mdl"),
        P(None, "mdl"),
        P("mdl", None),
        P(None, "tok", "mdl", None),
        P(None, "tok", "mdl", None),
        P("tok", None, "mdl", None),
        P("tok", None, "mdl", None),
        P("tok"),
        P(),
        P("tok", None, None),
        P("tok", None),
    )
    return jax.shard_map(
        shards,
        mesh=mesh,
        in_specs=placed,
        out_specs=(P("tok", "mdl"), P("tok", None, "mdl")),
        check_vma=False,
    )
```

profile of v0, /device:TPU:0, one launch (start us, length us, event | category | flops | bytes accessed | tf_op | source)
XLA Modules:
  0.0 233.8 jit_solution(10917397976916189196)
XLA Ops:
  7.2 0.7 all-gather.3.cloned.1.call-update
  8.0 0.7 all-gather.5.cloned.1.call-update
  8.7 0.7 convert_element_type.64
  9.4 2.3 %fusion.8 = f32[256]{0:T(256)S(1)} fusion(bf16[256,5120]{1,0:T(8,128)(2,1)} %param.16), kind=kLoop, calls=%fused_computation.22 | loop fusion | flops 3931904 | bytes 2622464 | tf_op jit(solution)/shard_map/reduce_sum | solution.py:91
  11.8 4.9 %fusion.66 = f32[256,512]{1,0:T(8,128)S(1)} fusion(bf16[5120,512]{1,0:T(8,128)(2,1)} %param.18, bf16[256,5120]{1,0:T(8,128)(2,1)} %param.16, f32[5120]{0:T(1024)S(1)} %convert_element_type.64, f32[256]{0:T(256)S(1)} %add_rsqrt_fusion), kind=kOutput, calls=%fused_computation.98 | convolution fusion | flops 1347420160 | bytes 8410112 | tf_op jit(solution)/shard_map/dot_general | solution.py:94
  16.7 0.2 reshape.339
  16.9 0.2 reduce_sum.66
  17.3 2.9 %convolution_bitcast_fusion.1 = f32[256,1,128]{0,2,1:T(8,128)S(1)} fusion(bf16[5120,128]{1,0:T(8,128)(2,1)S(1)} %copy-done, bf16[256,5120]{1,0:T(8,128)(2,1)} %param.16, f32[5120]{0:T(1024)S(1)} %convert_element_type.64, f32[256]{0:T(256)S(1)} %add_rsqrt_fusion), kind=kOutput, calls=%fused_computation.43 | convolution fusion | flops 340787200 | bytes 4084736 | tf_op jit(solution)/shard_map/dot_general | solution.py:97
  20.2 0.3 fusion.54
  21.0 0.5 multiply_cosine_fusion
  21.5 0.3 fusion.68
  21.9 0.1 subtract_convert_fusion
  22.0 0.1 pad_maximum_fusion
  22.2 0.6 fusion.69
  22.8 3.7 %convolution_convert_fusion.1 = bf16[256,128]{1,0:T(8,128)(2,1)S(1)} fusion(bf16[5120,128]{1,0:T(8,128)(2,1)} %param.20, bf16[256,5120]{1,0:T(8,128)(2,1)} %param.16, f32[5120]{0:T(1024)S(1)} %convert_element_type.64, f32[256]{0:T(256)S(1)} %add_rsqrt_fusion), kind=kOutput, calls=%fused_computation.44 | convolution fusion | flops 340819968 | bytes 4019200 | tf_op jit(solution)/shard_map/dot_general | solution.py:101
  26.6 5.2 %fusion.6 = (f32[8,32,4]{1,2,0:T(4,128)S(1)}, f32[8,32,4,2048]{3,1,2,0:T(8,128)}) fusion(pred[8,2048]{1,0:T(8,128)(4,1)S(1)} %iota_compare_fusion, bf16[8,2048,1,128]{3,1,2,0:T(8,128)(2,1)S(1)} %copy-done.2, bf16[8,32,4,128]{3,1,0,2:T(8,128)(2,1)S(1)} %pad_maximum_fusion), kind=kOutput, calls=%fused_computation.17 | convolution fusion | flops 543161344 | bytes 12865536 | tf_op jit(solution)/shard_map/ntkgd,nckd->ntkgc/dot_general | solution.py:48
  31.8 42.3 %all-gather.3.cloned.1.call-done = bf16[6,4096,1,128]{3,1,2,0:T(8,128)(2,1)} async-done(((bf16[6,256,1,128]{3,1,2,0:T(8,128)(2,1)}), bf16[6,4096,1,128]{3,1,2,0:T(8,128)(2,1)}) %all-gather.3.cloned.1.call-update) | async-done | bytes 6291472 | tf_op jit(solution)/shard_map/all_gather | solution.py:117
  74.1 7.6 %gather_fusion.1 = bf16[8,4096,128]{2,1,0:T(8,128)(2,1)} fusion(bf16[6,4096,128]{2,1,0:T(8,128)(2,1)} %bitcast.177, s32[1024]{0:T(1024)S(1)} %pad_clamp_fusion.1), kind=kCustom, calls=%fused_computation.clone | custom fusion | bytes 16777248 | tf_op jit(solution)/shard_map/jit(_take)/gather | solution.py:116
  81.7 55.5 %all-gather.5.cloned.1.call-done = bf16[6,4096,1,128]{3,1,2,0:T(8,128)(2,1)} async-done(((bf16[6,256,1,128]{3,1,2,0:T(8,128)(2,1)}), bf16[6,4096,1,128]{3,1,2,0:T(8,128)(2,1)}) %all-gather.5.cloned.1.call-update) | async-done | bytes 6291472 | tf_op jit(solution)/shard_map/all_gather | solution.py:120
  137.2 7.4 %gather_fusion.2 = bf16[8,4096,128]{2,1,0:T(8,128)(2,1)} fusion(bf16[6,4096,128]{2,1,0:T(8,128)(2,1)} %bitcast.178, s32[1024]{0:T(1024)S(1)} %pad_clamp_fusion.1), kind=kCustom, calls=%fused_computation.1.clone | custom fusion | bytes 16777248 | tf_op jit(solution)/shard_map/jit(_take)/gather | solution.py:119
  144.7 9.4 %bitcast_select_fusion.1 = (bf16[8,4096,1,128]{3,1,0,2:T(8,128)(2,1)}, bf16[8,4096,1,128]{3,1,0,2:T(8,128)(2,1)S(1)}) fusion(bf16[8,4096,128]{2,1,0:T(8,128)(2,1)} %gather_fusion.2, pred[8]{0:T(512)(128)(4,1)S(1)} %get-tuple-element.7, bf16[8,4096,128]{2,1,0:T(8,128)(2,1)} %gather_fusion.1), kind=kLoop, calls=%fused_computation.13 | loop fusion | flops 8388608 | bytes 33554440 | tf_op jit(solution)/shard_map/jit(_take)/select_n | solution.py:119
  154.1 7.9 %bitcast_reduce_fusion = (f32[8,32,4]{1,2,0:T(4,128)S(1)}, f32[8,32,4,16]{1,2,3,0:T(4,128)S(1)}, f32[8,16,256,32,4]{2,3,4,1,0:T(8,128)}) fusion(bf16[8,16,256,128,1]{3,2,4,1,0:T(8,128)(2,1)S(1)} %bitcast.176, bf16[8,32,4,128]{3,1,0,2:T(8,128)(2,1)S(1)} %pad_maximum_fusion), kind=kOutput, calls=%fused_computation.3 | convolution fusion | flops 1086307328 | bytes 25497600 | tf_op jit(solution)/shard_map/ntkgd,nsckd->ntkgsc/dot_general | solution.py:31
  162.0 10.1 %multiply_reduce_fusion = f32[8,32,4,128]{3,1,2,0:T(8,128)S(1)} fusion(f32[8,32,4,16]{1,2,3,0:T(4,128)S(1)} %get-tuple-element.4, bf16[8,16,256,128,1]{3,2,4,1,0:T(8,128)(2,1)} %bitcast.180, f32[8,16,256,32,4]{2,3,4,1,0:T(8,128)} %get-tuple-element.20), kind=kOutput, calls=%fused_computation.15 | convolution fusion | flops 1092485120 | bytes 25755648 | tf_op jit(solution)/shard_map/ntkgsc,nsckd->ntkgsd/dot_general | solution.py:36
  172.1 6.3 %fusion.31 = f32[8,32,1,4,128]{4,1,3,0,2:T(8,128)S(1)} fusion(bf16[8,2048,1,128]{3,1,2,0:T(8,128)(2,1)} %param.25, f32[8,32,4,2048]{3,1,2,0:T(8,128)} %get-tuple-element.24, pred[8,2048]{1,0:T(8,128)(4,1)S(1)} %iota_compare_fusion, f32[8,32,4,128]{3,1,2,0:T(8,128)S(1)} %multiply_reduce_fusion), kind=kOutput, calls=%fused_computation.40 | convolution fusion | flops 543293440 | bytes 13647872 | tf_op jit(solution)/shard_map/ntkgc,nckd->ntkgd/dot_general | solution.py:54
  178.4 0.3 fusion.36
  178.9 5.6 %convolution_convert_fusion = bf16[256,5120]{1,0:T(8,128)(2,1)} fusion(bf16[512,5120]{1,0:T(8,128)(2,1)} %param.21, bf16[32,8,4,128]{3,2,1,0:T(4,128)(2,1)S(1)} %bitcast.184), kind=kOutput, calls=%fused_computation.21 | convolution fusion | flops 1343488000 | bytes 8126464 | tf_op jit(solution)/shard_map/dot_general | solution.py:140
  184.5 4.4 %copy.47 = bf16[256,5120]{0,1:T(8,128)(2,1)} copy(bf16[256,5120]{1,0:T(8,128)(2,1)} %convolution_convert_fusion) | data formatting | bytes 5242880
  189.1 34.3 %reduce-scatter.4.cloned.1.call-done = bf16[640,256]{1,0:T(8,128)(2,1)} async-done(((bf16[5120,256]{1,0:T(8,128)(2,1)}), bf16[640,256]{1,0:T(8,128)(2,1)}) %reduce-scatter.4.cloned.1.call-update) | async-done | bytes 327696
  223.4 1.2 copy.48
  224.6 1.2 convert_add_fusion
  225.8 0.7 gather_fusion
  226.5 0.7 fusion.48
  (39 shorter events, 1.2 us)
Async XLA Ops:
  7.2 10.1 %copy-start = (bf16[5120,128]{1,0:T(8,128)(2,1)S(1)}, bf16[5120,128]{1,0:T(8,128)(2,1)}, u32[]{:S(2)}) copy-start(bf16[5120,128]{1,0:T(8,128)(2,1)} %param.19) | copy-start | bytes 3932164
  7.2 66.9 %all-gather.3.cloned.1.call-start = ((), (), s32[]{:S(2)}) async-start(), calls=%async_computation.1 | async-start | bytes 6684672 | tf_op jit(solution)/shard_map/all_gather | solution.py:117
  7.9 129.3 %all-gather.5.cloned.1.call-start = ((), (), s32[]{:S(2)}) async-start(), calls=%async_computation.2 | async-start | bytes 6684672 | tf_op jit(solution)/shard_map/all_gather | solution.py:120
  8.7 214.8 %reduce-scatter.4.cloned.1.call-start = ((), (), s32[]{:S(2)}) async-start(), calls=%async_computation.3 | async-start | bytes 2949120
  11.8 5.1 %copy-start.4 = (s32[8,32,32]{2,1,0:T(8,128)S(1)}, s32[8,32,32]{2,1,0:T(8,128)}, u32[]{:S(2)}) copy-start(s32[8,32,32]{2,1,0:T(8,128)} %param.28) | copy-start | bytes 98308
  11.8 5.3 %copy-start.6 = (s32[8]{0:T(128)S(1)}, s32[8]{0:T(128)}, u32[]{:S(2)}) copy-start(s32[8]{0:T(128)} %param.26) | copy-start | bytes 100
  16.7 4.2 %copy-start.7 = (s32[128]{0:T(128)S(1)}, s32[128]{0:T(128)}, u32[]{:S(2)}) copy-start(s32[128]{0:T(128)} %param.27) | copy-start | bytes 1540
  21.9 4.7 %copy-start.2 = (bf16[8,2048,1,128]{3,1,2,0:T(8,128)(2,1)S(1)}, bf16[8,2048,1,128]{3,1,2,0:T(8,128)(2,1)}, u32[]{:S(2)}) copy-start(bf16[8,2048,1,128]{3,1,2,0:T(8,128)(2,1)} %param.24) | copy-start | bytes 12582916
  178.9 48.4 %copy-start.1 = (bf16[5120,128]{1,0:T(8,128)(2,1)S(1)}, bf16[5120,128]{1,0:T(8,128)(2,1)}, u32[]{:S(2)}) copy-start(bf16[5120,128]{1,0:T(8,128)(2,1)} %param.19) | copy-start | bytes 3932164
  184.5 4.4 %copy-start.5 = (s32[8,8]{1,0:T(8,128)S(1)}, s32[8,8]{1,0:T(8,128)}, u32[]{:S(2)}) copy-start(s32[8,8]{1,0:T(8,128)} %param.29) | copy-start | bytes 772
  224.6 2.6 %copy-start.3 = (bf16[256,640]{1,0:T(8,128)(2,1)}, bf16[256,640]{1,0:T(8,128)(2,1)S(1)}, u32[]{:S(2)}) copy-start(bf16[256,640]{1,0:T(8,128)(2,1)S(1)} %copy.48) | copy-start | bytes 983044
Sparse Core Ops, SparseCore 0:
  10.1 63.9 all-gather.2
  76.2 60.9 all-gather.4
  189.0 34.3 reduce-scatter.3
where the time goes:
time: 234 us
  waiting for transfers between devices  134 us (57%)
  matrix products  47.5 us (20%)
  local copies, waits for them, and re-layouts  22.6 us (10%)
  other arithmetic  16.1 us (7%)
  between operations  14 us (6%)
    all_gather x1, waiting for transfers between devices, shards(): lax.all_gather(prompt_values, 'tok', axis=1, tiled=True)  55.5 us
    all_gather x1, waiting for transfers between devices, shards(): lax.all_gather(prompt_keys, 'tok', axis=1, tiled=True)  42.3 us
    unnamed x4, waiting for transfers between devices  35.7 us
    dot_general x1, matrix products, slice_attention(): jnp.einsum('ntkgsc,nsckd->ntkgsd', weights.astype(jnp.bfloat16), values_s...  10.1 us
    select_n x1, other arithmetic, shards(): jnp.take(lax.all_gather(prompt_values, 'tok', axis=1, tiled=True), own_gr...  9.37 us
    dot_general x1, matrix products, slice_attention(): jnp.einsum('ntkgd,nsckd->ntkgsc', grouped, keys_split, preferred_element_...  7.87 us
    gather x1, local copies, waits for them, and re-layouts, shards(): jnp.take(lax.all_gather(prompt_keys, 'tok', axis=1, tiled=True), own_grou...  7.64 us
    gather x1, local copies, waits for them, and re-layouts, shards(): jnp.take(lax.all_gather(prompt_values, 'tok', axis=1, tiled=True), own_gr...  7.44 us
  transfers between devices with their start and end apart: 3, of which 3 were waited for; matrix products, arithmetic and copies ran while one was open for 13% of the time, Pallas kernels for 0%

commit v1 on v0

--- a/solution.py
+++ b/solution.py
@@ -117,7 +117,11 @@
         lax.all_gather(prompt_keys, "tok", axis=1, tiled=True), own_groups, axis=0
     )
     chosen_values = jnp.take(
-        lax.all_gather(prompt_values, "tok", axis=1, tiled=True), own_groups, axis=0
+        jnp.concatenate(
+            lax.all_to_all(jnp.stack([prompt_values] * lax.axis_size("tok")), "tok", 0, 0), axis=1
+        ),
+        own_groups,
+        axis=0,
     )
     outputs, totals = slice_attention(grouped, chosen_keys, chosen_values, slice_rows, factor)
     weighted = jnp.sum(totals[..., None] * outputs.astype(jnp.float32), axis=4)

time: 234 us -> 242 us (1.034)
  waiting for transfers between devices: 134 us -> 122 us
  local copies, waits for them, and re-layouts: 22.6 us -> 34.1 us
  starting transfers between devices: 0.11 us -> 8.42 us
    all_to_all x0 -> x1, waiting for transfers between devices: none -> 86.8 us  [shards(): lax.all_to_all(jnp.stack([prompt_values] * lax.axis_size('tok')), 'tok',...]
    all_gather x1 -> x0, waiting for transfers between devices: 55.5 us -> none  [shards(): lax.all_gather(prompt_values, 'tok', axis=1, tiled=True)]
    all_gather x1, waiting for transfers between devices: 42.3 us -> 0.01 us  [shards(): lax.all_gather(prompt_keys, 'tok', axis=1, tiled=True)]
    all_to_all x0 -> x1, starting transfers between devices: none -> 8.34 us  [shards(): lax.all_to_all(jnp.stack([prompt_values] * lax.axis_size('tok')), 'tok',...]
    all_to_all x0 -> x1, local copies, waits for them, and re-layouts: none -> 6.29 us  [shards(): lax.all_to_all(jnp.stack([prompt_values] * lax.axis_size('tok')), 'tok',...]
    another operation x2 -> x3, local copies, waits for them, and re-layouts: 0.23 us -> 5.49 us  [the longest x1 5.26 us: shards(): jnp.stack([prompt_values] * lax.axis_size('tok'))]
    unnamed x4 -> x3, waiting for transfers between devices: 35.7 us -> 35.5 us
    unnamed x18 -> x20, local copies, waits for them, and re-layouts: 5.6 us -> 5.61 us
  transfers between devices with their start and end apart: 3 -> 3, of which waited for: 3 -> 2; matrix products, arithmetic and copies ran while one was open for 13% -> 17% of each run, Pallas kernels for 0% -> 0%
where the time goes in v1:
time: 242 us
  waiting for transfers between devices  122 us (50%)
  matrix products  47.2 us (20%)
  local copies, waits for them, and re-layouts  34.1 us (14%)
  other arithmetic  15.5 us (6%)
  between operations  14.3 us (6%)
  starting transfers between devices  8.42 us (3%)
    all_to_all x1, waiting for transfers between devices, shards(): lax.all_to_all(jnp.stack([prompt_values] * lax.axis_size('tok')), 'tok',...  86.8 us
    unnamed x3, waiting for transfers between devices  35.5 us
    dot_general x1, matrix products, slice_attention(): jnp.einsum('ntkgsc,nsckd->ntkgsd', weights.astype(jnp.bfloat16), values_s...  10.1 us
    select_n x1, other arithmetic, shards(): jnp.take(jnp.concatenate(lax.all_to_all(jnp.stack([prompt_values] * lax.a...  9.37 us
    all_to_all x1, starting transfers between devices, shards(): lax.all_to_all(jnp.stack([prompt_values] * lax.axis_size('tok')), 'tok',...  8.34 us
    dot_general x1, matrix products, slice_attention(): jnp.einsum('ntkgd,nsckd->ntkgsc', grouped, keys_split, preferred_element_...  7.87 us
    gather x1, local copies, waits for them, and re-layouts, shards(): jnp.take(jnp.concatenate(lax.all_to_all(jnp.stack([prompt_values] * lax.a...  7.62 us
    gather x1, local copies, waits for them, and re-layouts, shards(): jnp.take(lax.all_gather(prompt_keys, 'tok', axis=1, tiled=True), own_grou...  7.46 us
  transfers between devices with their start and end apart: 3, of which 2 were waited for; matrix products, arithmetic and copies ran while one was open for 17% of the time, Pallas kernels for 0%

profile of v1, /device:TPU:0, one launch (start us, length us, event | category | flops | bytes accessed | tf_op | source)
XLA Modules:
  0.0 241.8 jit_solution(16062100261828617529)
XLA Ops:
  7.2 0.7 all-gather.2.cloned.1.call-update
  7.9 5.3 %stack.2 = bf16[16,6,256,1,128]{4,2,1,3,0:T(8,128)(2,1)} broadcast(bf16[6,256,128]{2,1,0:T(8,128)(2,1)} %bitcast.188), dimensions={1,2,4} | broadcast | bytes 6684672 | tf_op jit(solution)/shard_map/stack | solution.py:121
  13.2 8.3 %all-to-all-start = ((bf16[16,6,256,1,128]{4,2,1,3,0:T(8,128)(2,1)}), bf16[16,6,256,1,128]{4,2,1,3,0:T(8,128)(2,1)}, u32[]{:S(2)}, u32[]{:S(2)}) async-start(bf16[16,6,256,1,128]{4,2,1,3,0:T(8,128)(2,1)} %stack.2), calls=%async_computation | async-start | bytes 12582912 | tf_op jit(solution)/shard_map/all_to_all | solution.py:121
  21.6 2.5 %fusion.8 = f32[256]{0:T(256)S(1)} fusion(bf16[256,5120]{1,0:T(8,128)(2,1)} %param.16), kind=kLoop, calls=%fused_computation.22 | loop fusion | flops 3931904 | bytes 2622464 | tf_op jit(solution)/shard_map/reduce_sum | solution.py:91
  24.1 4.9 %fusion.66 = f32[256,512]{1,0:T(8,128)S(1)} fusion(bf16[5120,512]{1,0:T(8,128)(2,1)} %param.18, bf16[256,5120]{1,0:T(8,128)(2,1)} %param.16, f32[5120]{0:T(1024)S(1)} %convert_element_type.64, f32[256]{0:T(256)S(1)} %add_rsqrt_fusion), kind=kOutput, calls=%fused_computation.98 | convolution fusion | flops 1347420160 | bytes 8410112 | tf_op jit(solution)/shard_map/dot_general | solution.py:94
  29.0 0.2 reshape.348
  29.2 0.2 reduce_sum.66
  29.6 2.9 %convolution_bitcast_fusion.1 = f32[256,1,128]{0,2,1:T(8,128)S(1)} fusion(bf16[5120,128]{1,0:T(8,128)(2,1)S(1)} %copy-done, bf16[256,5120]{1,0:T(8,128)(2,1)} %param.16, f32[5120]{0:T(1024)S(1)} %convert_element_type.64, f32[256]{0:T(256)S(1)} %add_rsqrt_fusion), kind=kOutput, calls=%fused_computation.43 | convolution fusion | flops 340787200 | bytes 4084736 | tf_op jit(solution)/shard_map/dot_general | solution.py:97
  32.5 0.3 fusion.54
  33.4 0.5 multiply_cosine_fusion
  33.9 0.3 fusion.68
  34.2 0.1 subtract_convert_fusion
  34.4 0.1 pad_maximum_fusion
  34.5 0.6 fusion.69
  35.1 3.4 %convolution_convert_fusion.1 = bf16[256,128]{1,0:T(8,128)(2,1)S(1)} fusion(bf16[5120,128]{1,0:T(8,128)(2,1)} %param.20, bf16[256,5120]{1,0:T(8,128)(2,1)} %param.16, f32[5120]{0:T(1024)S(1)} %convert_element_type.64, f32[256]{0:T(256)S(1)} %add_rsqrt_fusion), kind=kOutput, calls=%fused_computation.44 | convolution fusion | flops 340819968 | bytes 4019200 | tf_op jit(solution)/shard_map/dot_general | solution.py:101
  38.7 5.2 %fusion.6 = (f32[8,32,4]{1,2,0:T(4,128)S(1)}, f32[8,32,4,2048]{3,1,2,0:T(8,128)}) fusion(pred[8,2048]{1,0:T(8,128)(4,1)S(1)} %iota_compare_fusion, bf16[8,2048,1,128]{3,1,2,0:T(8,128)(2,1)S(1)} %copy-done.2, bf16[8,32,4,128]{3,1,0,2:T(8,128)(2,1)S(1)} %pad_maximum_fusion), kind=kOutput, calls=%fused_computation.17 | convolution fusion | flops 543161344 | bytes 12865536 | tf_op jit(solution)/shard_map/ntkgd,nckd->ntkgc/dot_general | solution.py:48
  43.9 86.8 %all-to-all-done = bf16[16,6,256,1,128]{4,2,1,3,0:T(8,128)(2,1)} async-done(((bf16[16,6,256,1,128]{4,2,1,3,0:T(8,128)(2,1)}), bf16[16,6,256,1,128]{4,2,1,3,0:T(8,128)(2,1)}, u32[]{:S(2)}, u32[]{:S(2)}) %all-to-all-start) | async-done | bytes 6291488 | tf_op jit(solution)/shard_map/all_to_all | solution.py:121
  130.6 6.3 %copy.33 = bf16[16,6,256,1,128]{4,2,0,1,3:T(8,128)(2,1)} copy(bf16[16,6,256,1,128]{4,2,1,3,0:T(8,128)(2,1)} %all-to-all-done) | data formatting | bytes 12582912 | tf_op jit(solution)/shard_map/all_to_all | solution.py:121
  136.9 7.6 %gather_fusion.2 = bf16[8,4096,128]{2,1,0:T(8,128)(2,1)} fusion(bf16[6,4096,128]{2,1,0:T(8,128)(2,1)} %bitcast.182, s32[1024]{0:T(1024)S(1)} %pad_clamp_fusion.1), kind=kCustom, calls=%fused_computation.1.clone | custom fusion | bytes 16777248 | tf_op jit(solution)/shard_map/jit(_take)/gather | solution.py:119
  144.6 7.5 %gather_fusion.1 = bf16[8,4096,128]{2,1,0:T(8,128)(2,1)} fusion(bf16[6,4096,128]{2,1,0:T(8,128)(2,1)} %bitcast.183, s32[1024]{0:T(1024)S(1)} %pad_clamp_fusion.1), kind=kCustom, calls=%fused_computation.clone | custom fusion | bytes 16777248 | tf_op jit(solution)/shard_map/jit(_take)/gather | solution.py:116
  152.0 9.4 %bitcast_select_fusion.1 = (bf16[8,4096,1,128]{3,1,0,2:T(8,128)(2,1)}, bf16[8,4096,1,128]{3,1,0,2:T(8,128)(2,1)S(1)}) fusion(bf16[8,4096,128]{2,1,0:T(8,128)(2,1)} %gather_fusion.2, pred[8]{0:T(512)(128)(4,1)S(1)} %get-tuple-element.7, bf16[8,4096,128]{2,1,0:T(8,128)(2,1)} %gather_fusion.1), kind=kLoop, calls=%fused_computation.13 | loop fusion | flops 8388608 | bytes 33554440 | tf_op jit(solution)/shard_map/jit(_take)/select_n | solution.py:119
  161.4 7.9 %bitcast_reduce_fusion = (f32[8,32,4]{1,2,0:T(4,128)S(1)}, f32[8,32,4,16]{1,2,3,0:T(4,128)S(1)}, f32[8,16,256,32,4]{2,3,4,1,0:T(8,128)}) fusion(bf16[8,16,256,128,1]{3,2,4,1,0:T(8,128)(2,1)S(1)} %bitcast.181, bf16[8,32,4,128]{3,1,0,2:T(8,128)(2,1)S(1)} %pad_maximum_fusion), kind=kOutput, calls=%fused_computation.3 | convolution fusion | flops 1086307328 | bytes 25497600 | tf_op jit(solution)/shard_map/ntkgd,nsckd->ntkgsc/dot_general | solution.py:31
  169.3 10.1 %multiply_reduce_fusion = f32[8,32,4,128]{3,1,2,0:T(8,128)S(1)} fusion(f32[8,32,4,16]{1,2,3,0:T(4,128)S(1)} %get-tuple-element.4, bf16[8,16,256,128,1]{3,2,4,1,0:T(8,128)(2,1)} %bitcast.185, f32[8,16,256,32,4]{2,3,4,1,0:T(8,128)} %get-tuple-element.20), kind=kOutput, calls=%fused_computation.15 | convolution fusion | flops 1092485120 | bytes 25755648 | tf_op jit(solution)/shard_map/ntkgsc,nsckd->ntkgsd/dot_general | solution.py:36
  179.4 6.3 %fusion.31 = f32[8,32,1,4,128]{4,1,3,0,2:T(8,128)S(1)} fusion(bf16[8,2048,1,128]{3,1,2,0:T(8,128)(2,1)} %param.25, f32[8,32,4,2048]{3,1,2,0:T(8,128)} %get-tuple-element.24, pred[8,2048]{1,0:T(8,128)(4,1)S(1)} %iota_compare_fusion, f32[8,32,4,128]{3,1,2,0:T(8,128)S(1)} %multiply_reduce_fusion), kind=kOutput, calls=%fused_computation.40 | convolution fusion | flops 543293440 | bytes 13647872 | tf_op jit(solution)/shard_map/ntkgc,nckd->ntkgd/dot_general | solution.py:54
  185.7 0.3 fusion.36
  186.2 5.6 %convolution_convert_fusion = bf16[256,5120]{1,0:T(8,128)(2,1)} fusion(bf16[512,5120]{1,0:T(8,128)(2,1)} %param.21, bf16[32,8,4,128]{3,2,1,0:T(4,128)(2,1)S(1)} %bitcast.190), kind=kOutput, calls=%fused_computation.21 | convolution fusion | flops 1343488000 | bytes 8126464 | tf_op jit(solution)/shard_map/dot_general | solution.py:144
  191.8 4.4 %copy.48 = bf16[256,5120]{0,1:T(8,128)(2,1)} copy(bf16[256,5120]{1,0:T(8,128)(2,1)} %convolution_convert_fusion) | data formatting | bytes 5242880
  196.4 34.8 %reduce-scatter.4.cloned.1.call-done = bf16[640,256]{1,0:T(8,128)(2,1)} async-done(((bf16[5120,256]{1,0:T(8,128)(2,1)}), bf16[640,256]{1,0:T(8,128)(2,1)}) %reduce-scatter.4.cloned.1.call-update) | async-done | bytes 327696
  231.2 1.2 copy.49
  232.4 1.2 convert_add_fusion
  233.6 0.7 gather_fusion
  234.3 0.7 fusion.48
  (42 shorter events, 1.2 us)
Async XLA Ops:
  7.2 22.4 %copy-start = (bf16[5120,128]{1,0:T(8,128)(2,1)S(1)}, bf16[5120,128]{1,0:T(8,128)(2,1)}, u32[]{:S(2)}) copy-start(bf16[5120,128]{1,0:T(8,128)(2,1)} %param.19) | copy-start | bytes 3932164
  7.2 137.4 %all-gather.2.cloned.1.call-start = ((), (), s32[]{:S(2)}) async-start(), calls=%async_computation.2 | async-start | bytes 6684672 | tf_op jit(solution)/shard_map/all_gather | solution.py:117
  13.2 8.4 %copy-start.5 = (bf16[5120]{0:T(1024)(128)(2,1)S(1)}, bf16[5120]{0:T(1024)(128)(2,1)}, u32[]{:S(2)}) copy-start(bf16[5120]{0:T(1024)(128)(2,1)} %param.17) | copy-start | bytes 30724
  13.2 117.5 %all-to-all-start = ((bf16[16,6,256,1,128]{4,2,1,3,0:T(8,128)(2,1)}), bf16[16,6,256,1,128]{4,2,1,3,0:T(8,128)(2,1)}, u32[]{:S(2)}, u32[]{:S(2)}) async-start(bf16[16,6,256,1,128]{4,2,1,3,0:T(8,128)(2,1)} %stack.2), calls=%async_computation | async-start | bytes 12582912 | tf_op jit(solution)/shard_map/all_to_all | solution.py:121
  21.5 209.7 %reduce-scatter.4.cloned.1.call-start = ((), (), s32[]{:S(2)}) async-start(), calls=%async_computation.3 | async-start | bytes 2949120
  24.1 5.1 %copy-start.4 = (s32[8,32,32]{2,1,0:T(8,128)S(1)}, s32[8,32,32]{2,1,0:T(8,128)}, u32[]{:S(2)}) copy-start(s32[8,32,32]{2,1,0:T(8,128)} %param.28) | copy-start | bytes 98308
  24.1 5.3 %copy-start.7 = (s32[8]{0:T(128)S(1)}, s32[8]{0:T(128)}, u32[]{:S(2)}) copy-start(s32[8]{0:T(128)} %param.26) | copy-start | bytes 100
  29.0 4.2 %copy-start.8 = (s32[128]{0:T(128)S(1)}, s32[128]{0:T(128)}, u32[]{:S(2)}) copy-start(s32[128]{0:T(128)} %param.27) | copy-start | bytes 1540
  34.2 4.4 %copy-start.2 = (bf16[8,2048,1,128]{3,1,2,0:T(8,128)(2,1)S(1)}, bf16[8,2048,1,128]{3,1,2,0:T(8,128)(2,1)}, u32[]{:S(2)}) copy-start(bf16[8,2048,1,128]{3,1,2,0:T(8,128)(2,1)} %param.24) | copy-start | bytes 12582916
  186.2 48.8 %copy-start.1 = (bf16[5120,128]{1,0:T(8,128)(2,1)S(1)}, bf16[5120,128]{1,0:T(8,128)(2,1)}, u32[]{:S(2)}) copy-start(bf16[5120,128]{1,0:T(8,128)(2,1)} %param.19) | copy-start | bytes 3932164
  191.8 4.4 %copy-start.6 = (s32[8,8]{1,0:T(8,128)S(1)}, s32[8,8]{1,0:T(8,128)}, u32[]{:S(2)}) copy-start(s32[8,8]{1,0:T(8,128)} %param.29) | copy-start | bytes 772
  232.4 2.6 %copy-start.3 = (bf16[256,640]{1,0:T(8,128)(2,1)}, bf16[256,640]{1,0:T(8,128)(2,1)S(1)}, u32[]{:S(2)}) copy-start(bf16[256,640]{1,0:T(8,128)(2,1)S(1)} %copy.49) | copy-start | bytes 983044
Sparse Core Ops, SparseCore 0:
  10.1 133.8 all-gather.1
  196.4 34.7 reduce-scatter.3
